TPU v7x, 32 devices: a whole 2x2x4 slice. The times are simulated.
32 devices in a mesh: parts: 2 (over x), pts: 16 (over z, y, core).
Axes of the slice: x: 2, y: 2, z: 4, core: 2. Of those that a mesh axis runs over, the one named last changes fastest.
Arguments:
- grid_weights: float32 [256, 128, 128], P(('parts', 'pts')), parts along dimension 0, may hold values from -6 to 6
- direction: float32 [256, 128, 128], P(('parts', 'pts')), parts along dimension 0, may hold values from -6 to 6
- kern_x: float32 [128, 128], replicated
- kern_y: float32 [128, 128], replicated
- kern_z: float32 [128, 128], replicated
- interp: bfloat16 [4096, 128, 256], P(('parts', 'pts')), parts along dimension 0, may hold values from -4 to 4
- block_corner: int32 [3, 4096], P(None, ('parts', 'pts')), parts along dimension 1, may hold values from 0 to 120, as said below
- block_offsets: int32 [4096, 256], P(('parts', 'pts')), parts along dimension 0, may hold values from 0 to 2047, as said below
- labels: int32 [4096, 128], P(('parts', 'pts')), parts along dimension 0, may hold values 0 or 1
- trial_steps: float32 [5], replicated, may hold values from 0.05 to 2
- accept: int32 [1], replicated, may hold values from 0 to 4
Outputs:
- new_weights: float32 [256, 128, 128], P(('parts', 'pts')), parts along dimension 0
- grid_gradient: float32 [256, 128, 128], P(('parts', 'pts')), parts along dimension 0
- curvature: float32 [4096, 128], P(('parts', 'pts')), parts along dimension 0
- trial_objective: float32 [10], P('parts'), parts along dimension 0
- trial_slope: float32 [10], P('parts'), parts along dimension 0
There are 2 independent parts, one for each index of `parts`. A program takes and returns all parts, laid end to end along the dimension named above; an argument that names none is the same for every part. Nothing has to cross between parts.
Inputs may be any that keep to these rules, and one draw needn't show every extreme that they name: `block_corner`: row 0 lies in 0 to 112, row 1 in 0 to 112, row 2 in 0 to 120. `block_offsets`: the 256 offsets of one block are distinct.
All inputs are finite; a program needn't handle non-finite values. No bound on the sum of `labels` on one device may be relied on, other than what follows from the above.
Results may differ from a plain program's by a relative error of at most 0.0075.
The roundings to bfloat16 on the way count: a program that leaves them out, or rounds other values in their place, can miss the bound.
Values may be sent and summed in bfloat16 or wider, within the bound.
A program may use at most 128 MiB of HBM per device.

v0:
```python
import jax
import jax.numpy as jnp
from jax import lax
from jax.sharding import PartitionSpec as P

BOXY = 16
BOXZ = 8
NTRIAL = 5
HIGHEST = lax.Precision.HIGHEST


def plane_mix(fields, kern_y, kern_z):
    inner_mix = jnp.einsum("...bc,zc->...bz", fields, kern_z, precision=HIGHEST)
    return jnp.einsum("...xbz,yb->...xyz", inner_mix, kern_y, precision=HIGHEST).astype(
        jnp.bfloat16
    )


def depth_mix(partial_value, kern_x):
    return jnp.einsum(
        "xa,...ayz->...xyz", kern_x, partial_value.astype(jnp.float32), precision=HIGHEST
    )


def cell_parts_of(block_corner, block_offsets, size_y):
    plane_off = block_offsets // (BOXY * BOXZ)
    row_off = block_offsets // BOXZ % BOXY
    depth_off = block_offsets % BOXZ
    cell_x = block_corner[0][:, None] + plane_off
    cell_y = block_corner[1][:, None] + row_off
    cell_z = block_corner[2][:, None] + depth_off
    return (cell_x * size_y + cell_y, cell_z)


def pick_cells(grid_rows, row_ids, depth_ids):
    depth_size = grid_rows.shape[-1]
    taken = jnp.take(grid_rows, row_ids, axis=1)
    depth_line = lax.broadcasted_iota(jnp.int32, (1, 1, depth_size), 2)
    wanted = depth_ids[:, :, None] == depth_line
    kept = jnp.where(wanted[None], taken, jnp.zeros((), taken.dtype))
    return jnp.sum(kept.astype(jnp.float32), axis=-1).astype(jnp.bfloat16)


def slab_add(row_ids, depth_ids, flat_terms, row_count, size_y, size_z):
    inside = (row_ids >= 0) & (row_ids < row_count * size_y)
    target_row = jnp.where(inside, row_ids, row_count * size_y)
    depth_line = lax.broadcasted_iota(jnp.int32, (1, size_z), 1)
    placed = jnp.where(depth_ids[:, None] == depth_line, flat_terms[:, None], 0.0)
    summed = (
        jnp.zeros((row_count * size_y, size_z), jnp.float32).at[target_row].add(placed, mode="drop")
    )
    return summed.reshape(row_count, size_y, size_z)


def kron_apply(fields, kern_x, kern_y, kern_z):
    partial_value = plane_mix(fields, kern_y, kern_z)
    slab_rows = fields.shape[1]
    gathered = lax.all_gather(partial_value, "pts", axis=1, tiled=True)
    mixed_grid = depth_mix(gathered, kern_x)
    slab_part = lax.dynamic_slice_in_dim(
        mixed_grid, lax.axis_index("pts") * slab_rows, slab_rows, 1
    )
    return (slab_part, mixed_grid.astype(jnp.bfloat16))


def body(
    grid_weights,
    direction,
    kern_x,
    kern_y,
    kern_z,
    interp,
    block_corner,
    block_offsets,
    labels,
    trial_steps,
    accept,
):
    slab_rows, size_y, size_z = grid_weights.shape
    devices = lax.axis_size("pts")
    points = interp.shape[0] * interp.shape[1] * devices
    row_ids, depth_ids = cell_parts_of(block_corner, block_offsets, size_y)
    slab_pair, whole_pair = kron_apply(jnp.stack([grid_weights, direction]), kern_x, kern_y, kern_z)
    quad_local = jnp.stack(
        [
            jnp.sum(grid_weights * slab_pair[0]),
            jnp.sum(direction * slab_pair[0]),
            jnp.sum(direction * slab_pair[1]),
        ]
    )
    quadratics = lax.psum(quad_local, "pts")
    values = pick_cells(whole_pair.reshape(2, -1, size_z), row_ids, depth_ids)
    latent_pair = jnp.einsum("bpc,fbc->fbp", interp, values, preferred_element_type=jnp.float32)
    latent = latent_pair[0]
    slope_pt = latent_pair[1]
    target = labels.astype(jnp.float32)
    signed = 2.0 * target - 1.0
    trial_latent = latent[None] + trial_steps[:, None, None] * slope_pt[None]
    loglik_local = jnp.sum(jax.nn.log_sigmoid(signed[None] * trial_latent), axis=(1, 2))
    descent_local = jnp.sum(
        (target[None] - jax.nn.sigmoid(trial_latent)) * slope_pt[None], axis=(1, 2)
    )
    loglik, descent = lax.psum((loglik_local, descent_local), "pts")
    prior = 0.5 * (
        quadratics[0]
        + 2.0 * trial_steps * quadratics[1]
        + trial_steps * trial_steps * quadratics[2]
    )
    trial_objective = (loglik - prior) / points
    trial_slope = (descent - quadratics[1] - trial_steps * quadratics[2]) / points
    chosen = jnp.sum(jnp.where(jnp.arange(NTRIAL) == accept[0], trial_steps, 0.0))
    probability = jax.nn.sigmoid(latent + chosen * slope_pt)
    residual = (target - probability).astype(jnp.bfloat16)
    column_term = jnp.einsum("bpc,bp->bc", interp, residual, preferred_element_type=jnp.float32)
    flat_rows = row_ids.reshape(-1)
    flat_depths = depth_ids.reshape(-1)
    flat_terms = column_term.reshape(-1)
    spread = lax.psum_scatter(
        slab_add(
            flat_rows, flat_depths, flat_terms, slab_rows * lax.axis_size("pts"), size_y, size_z
        ),
        "pts",
        scatter_dimension=0,
        tiled=True,
    )
    new_weights = grid_weights + chosen * direction
    grid_gradient = spread - new_weights
    unused_slab, bend_whole = kron_apply(grid_gradient[None], kern_x, kern_y, kern_z)
    bend_values = pick_cells(bend_whole.reshape(1, -1, size_z), row_ids, depth_ids)
    bend_pt = jnp.einsum("bpc,fbc->fbp", interp, bend_values, preferred_element_type=jnp.float32)[0]
    curvature = probability * (1.0 - probability) * bend_pt
    return (new_weights, grid_gradient, curvature, trial_objective, trial_slope)


def solution(mesh):
    return jax.shard_map(
        body,
        mesh=mesh,
        in_specs=(
            P(("parts", "pts"), None, None),
            P(("parts", "pts"), None, None),
            P(),
            P(),
            P(),
            P(("parts", "pts"), None, None),
            P(None, ("parts", "pts")),
            P(("parts", "pts"), None),
            P(("parts", "pts"), None),
            P(),
            P(),
        ),
        out_specs=(
            P(("parts", "pts"), None, None),
            P(("parts", "pts"), None, None),
            P(("parts", "pts"), None),
            P("parts"),
            P("parts"),
        ),
        check_vma=False,
    )
```

profile of v0, /device:TPU:0, one launch (start us, length us, event | category | flops | bytes accessed | tf_op | source)
XLA Modules:
  0.0 985.0 jit_solution(7694529611736947677)
XLA Ops:
  7.2 0.0 copy-start
  7.2 0.0 all-gather.3.cloned.1.call-start
  7.2 2.3 fusion.21
  9.5 2.6 fusion.16
  12.1 0.0 all-gather.3.cloned.1.call-update
  12.1 0.0 reduce-scatter.2.cloned.1.call-start
  12.8 0.8 slice_bitcast_fusion.2
  13.6 1.0 fusion.66
  14.6 0.1 copy.67
  14.7 1.2 compare_and_fusion
  15.9 0.1 copy.66
  16.0 0.1 copy.68
  16.1 1.3 fusion.53
  17.4 1.0 fusion.35
  18.4 6.9 iota_compare_fusion.1
  25.4 0.2 compare_select_fusion.1
  25.6 63.7 %all-gather.3.cloned.1.call-done = bf16[2,128,128,128]{2,3,1,0:T(8,128)(2,1)} async-done(((bf16[2,8,128,128]{2,3,1,0:T(8,128)(2,1)}), bf16[2,128,128,128]{2,3,1,0:T(8,128)(2,1)}) %all-gather.3.cloned.1.call-update) | async-done | bytes 8388624 | tf_op jit(solution)/shard_map/all_gather | solution.py:58
  89.3 12.4 %copy.43 = bf16[2,128,128,128]{3,1,2,0:T(8,128)(2,1)} copy(bf16[2,128,128,128]{2,3,1,0:T(8,128)(2,1)} %all-gather.3.cloned.1.call-done) | data formatting | bytes 16777216 | tf_op jit(solution)/shard_map/all_gather | solution.py:58
  101.8 0.0 copy-done
  101.8 9.8 fusion.42
  111.6 0.0 copy-start.1
  111.6 5.7 copy-done.1
  117.3 4.1 convert_bitcast_fusion
  121.3 12.0 %copy.44 = bf16[2,128,128,128]{3,2,1,0:T(8,128)(2,1)} copy(bf16[2,128,128,128]{3,1,2,0:T(8,128)(2,1)} %convert_bitcast_fusion) | data formatting | bytes 16777216 | tf_op jit(solution)/shard_map/convert_element_type | solution.py:63
  133.3 16.4 %copy.45 = bf16[2,16384,128]{2,0,1:T(2,128)(2,1)} copy(bf16[2,16384,128]{2,1,0:T(8,128)(2,1)} %bitcast.121) | data formatting | bytes 16777216 | tf_op jit(solution)/shard_map/reshape | solution.py:92
  149.7 214.5 %gather_fusion = bf16[32768,2,128]{2,1,0:T(2,128)(2,1)} fusion(bf16[2,16384,128]{2,0,1:T(2,128)(2,1)} %copy.45, s32[32768]{0:T(1024)S(1)} %broadcast_clamp_fusion), kind=kCustom, calls=%fused_computation | custom fusion | bytes 33685504 | tf_op jit(solution)/shard_map/jit(_take)/gather | solution.py:37
  364.3 97.9 %fusion.2 = bf16[128,256,2]{2,1,0:T(8,128)(2,1)} fusion(bf16[128,256,2,128]{3,2,1,0:T(2,128)(2,1)} %bitcast.118, pred[128,256]{1,0:T(8,128)(4,1)S(1)} %get-tuple-element.15, pred[128,256,128]{2,1,0:T(8,128)(4,1)} %iota_compare_fusion.1), kind=kLoop, calls=%fused_computation.10 | loop fusion | flops 25100288 | bytes 21135360 | tf_op jit(solution)/shard_map/reduce_sum | solution.py:41
  462.1 8.1 fusion.18
  470.2 0.1 fusion.57
  470.4 0.0 copy-done.6
  470.4 0.7 multiply_add_fusion.2
  471.0 4.6 fusion.50
  475.6 0.1 copy.69
  475.7 0.0 copy-start.2
  475.7 0.0 copy-start.3
  475.7 0.0 copy-start.5
  475.7 0.0 copy-start.7
  475.8 198.6 %scatter_custom_fusion = f32[16384,128]{1,0:T(8,128)} fusion(s32[32768]{0:T(1024)S(1)} %bitcast.138, f32[]{:T(128)} %constant.89.clone.1, f32[32768]{0:T(1024)S(1)} %bitcast.133, s32[32768]{0:T(1024)S(1)} %bitcast.132), kind=kCustom, calls=%fused_computation.6 | custom fusion | flops 12582912 | bytes 8651776 | tf_op jit(solution)/shard_map/scatter-add | solution.py:50
  674.4 0.0 reduce-scatter.2.cloned.1.call-update
  674.4 0.0 all-gather.5.cloned.1.call-start
  674.5 102.2 %reduce-scatter.2.cloned.1.call-done = f32[8,128,128]{2,1,0:T(8,128)} async-done(((f32[128,128,128]{2,1,0:T(8,128)}), f32[8,128,128]{2,1,0:T(8,128)}) %reduce-scatter.2.cloned.1.call-update) | async-done | bytes 524304 | tf_op jit(solution)/shard_map/reduce_scatter | solution.py:118
  776.6 0.0 copy-done.2
  776.6 0.0 copy-done.3
  776.6 2.5 fusion.55
  779.2 0.0 copy-done.5
  779.2 0.6 fusion.48
  779.8 0.6 fusion.17
  780.4 0.8 copy.49
  781.2 0.0 all-gather.5.cloned.1.call-update
  781.3 0.0 copy-done.8
  781.3 0.5 multiply_reduce_fusion.1
  781.8 1.3 dynamic-slice_bitcast_fusion
  783.1 1.3 multiply_reduce_fusion
  784.3 2.0 pad_maximum_fusion
  786.3 33.4 %all-reduce = (f32[5]{0:T(128)S(1)}, f32[3]{0:T(128)S(1)}, f32[5]{0:T(128)S(1)}) all-reduce(f32[5]{0:T(128)S(1)} %neg.22, f32[3]{0:T(128)S(1)} %pad_maximum_fusion, f32[5]{0:T(128)S(1)} %get-tuple-element.8), channel_id=1, replica_groups=mesh['parts'=2,'pts'=16] {'pts'}, use_global_device_ids=true, to_apply=%region_6.7 | all-reduce | flops 13 | bytes 104 | tf_op jit(solution)/shard_map/psum | solution.py:103
  819.7 0.7 fusion.58
  821.0 2.4 subtract_multiply_fusion.1
  823.4 8.2 all-gather.5.cloned.1.call-done
  831.5 7.2 convert_bitcast_fusion.1
  838.8 4.7 copy.51
  843.4 112.1 %gather_fusion.1 = bf16[32768,128]{1,0:T(8,128)(2,1)} fusion(bf16[16384,128]{1,0:T(8,128)(2,1)} %bitcast.117, s32[32768]{0:T(1024)S(1)} %broadcast_clamp_fusion), kind=kCustom, calls=%fused_computation.1 | custom fusion | bytes 16908288 | tf_op jit(solution)/shard_map/jit(_take)/gather | solution.py:37
  955.6 15.7 %fusion.4 = bf16[128,256]{1,0:T(8,128)(2,1)S(1)} fusion(bf16[1,128,256,128]{3,2,1,0:T(8,128)(2,1)} %bitcast.119, s32[128,256]{1,0:T(8,128)S(1)} %fusion.35, pred[128,256]{1,0:T(8,128)(4,1)S(1)} %get-tuple-element.15), kind=kLoop, calls=%fused_computation.12 | loop fusion | flops 16744448 | bytes 8617984 | tf_op jit(solution)/shard_map/reduce_sum | solution.py:41
  971.3 5.6 fusion.36
  977.0 1.3 fusion.41
  (10 shorter events, 0.1 us)
Async XLA Ops:
  7.2 94.6 %copy-start = (f32[128,128]{1,0:T(8,128)S(1)}, f32[128,128]{1,0:T(8,128)}, u32[]{:S(2)}) copy-start(f32[128,128]{1,0:T(8,128)} %param.13) | copy-start | bytes 196612
  7.2 82.2 %all-gather.3.cloned.1.call-start = ((), (), s32[]{:S(2)}) async-start(), calls=%async_computation.1 | async-start | bytes 8912896 | tf_op jit(solution)/shard_map/all_gather | solution.py:58
  12.1 764.5 %reduce-scatter.2.cloned.1.call-start = ((), (), s32[]{:S(2)}) async-start(), calls=%async_computation.2 | async-start | bytes 8912896 | tf_op jit(solution)/shard_map/reduce_scatter | solution.py:118
  111.6 5.7 copy-start.1
  462.1 8.2 copy-start.6
  475.7 300.9 %copy-start.2 = (f32[8,128,128]{2,1,0:T(8,128)S(1)}, f32[8,128,128]{2,1,0:T(8,128)}, u32[]{:S(2)}) copy-start(f32[8,128,128]{2,1,0:T(8,128)} %param.12) | copy-start | bytes 1572868
  475.7 300.9 %copy-start.3 = (f32[8,128,128]{2,1,0:T(8,128)S(1)}, f32[8,128,128]{2,1,0:T(8,128)}, u32[]{:S(2)}) copy-start(f32[8,128,128]{2,1,0:T(8,128)} %param.11) | copy-start | bytes 1572868
  475.7 303.5 %copy-start.5 = (f32[128,128]{1,0:T(8,128)S(1)}, f32[128,128]{1,0:T(8,128)}, u32[]{:S(2)}) copy-start(f32[128,128]{1,0:T(8,128)} %param.15) | copy-start | bytes 196612
  475.7 304.1 %copy-start.7 = (f32[128,128]{1,0:T(8,128)S(1)}, f32[128,128]{1,0:T(8,128)}, u32[]{:S(2)}) copy-start(f32[128,128]{1,0:T(8,128)} %param.14) | copy-start | bytes 196612
  674.4 106.9 %copy-start.8 = (f32[5]{0:T(128)S(1)}, f32[5]{0:T(128)}, u32[]{:S(2)}) copy-start(f32[5]{0:T(128)} %param.20) | copy-start | bytes 64
  674.4 157.1 %all-gather.5.cloned.1.call-start = ((), (), s32[]{:S(2)}) async-start(), calls=%async_computation.3 | async-start | bytes 4456448 | tf_op jit(solution)/shard_map/all_gather | solution.py:58
  779.2 64.3 %copy-start.4 = (f32[8,128,128]{2,1,0:T(8,128)}, f32[8,128,128]{2,1,0:T(8,128)S(1)}, u32[]{:S(2)}) copy-start(f32[8,128,128]{2,1,0:T(8,128)S(1)} %get-tuple-element.13) | copy-start | bytes 1572868
Sparse Core Ops, SparseCore 0:
  12.3 77.0 all-gather.2
  674.6 102.0 reduce-scatter.1
  781.4 50.1 all-gather.4
where the time goes:
time: 989 us; the launch traced here: 985 us
  local copies, waits for them, and re-layouts  382 us (39%)
  other arithmetic  339 us (34%)
  waiting for transfers between devices  174 us (18%)
  matrix products  41.3 us (4%)
  blocking collectives  33.4 us (3%)
  between operations  15.4 us (2%)
    gather x2, local copies, waits for them, and re-layouts, pick_cells(): taken = jnp.take(grid_rows, row_ids, axis=1)  327 us
    scatter-add x1, other arithmetic, slab_add(): jnp.zeros((row_count * size_y, size_z), jnp.float32).at[target_row]  199 us
    reduce_sum x2, other arithmetic, pick_cells(): return jnp.sum(kept.astype(jnp.float32), axis=-1).astype(jnp.bfloat16)  114 us
    reduce_scatter x1, waiting for transfers between devices, body(): lax.psum_scatter(slab_add(flat_rows, flat_depths, flat_terms, slab_rows *...  102 us
    all_gather x2, waiting for transfers between devices, kron_apply(): gathered = lax.all_gather(partial_value, 'pts', axis=1, tiled=True)  71.9 us
    psum x1, blocking collectives, body(): loglik, descent = lax.psum((loglik_local, descent_local), 'pts')  33.4 us
  transfers between devices with their start and end apart: 3, of which 3 were waited for; matrix products, arithmetic and copies ran while one was open for 2% of the time, Pallas kernels for 0%

commit v1 on v0

--- a/solution.py
+++ b/solution.py
@@ -55,7 +55,12 @@
 def kron_apply(fields, kern_x, kern_y, kern_z):
     partial_value = plane_mix(fields, kern_y, kern_z)
     slab_rows = fields.shape[1]
-    gathered = lax.all_gather(partial_value, "pts", axis=1, tiled=True)
+    ring = [partial_value]
+    for hop in range(15):
+        ring.append(lax.ppermute(ring[-1], "pts", [(dev, (dev + 1) % 16) for dev in range(16)]))
+    gathered = jnp.roll(
+        jnp.concatenate(ring[::-1], axis=1), (lax.axis_index("pts") + 1) * ring[0].shape[1], axis=1
+    )
     mixed_grid = depth_mix(gathered, kern_x)
     slab_part = lax.dynamic_slice_in_dim(
         mixed_grid, lax.axis_index("pts") * slab_rows, slab_rows, 1

time: 989 us -> 1280 us (1.29)
  waiting for transfers between devices: 174 us -> 368 us
  local copies, waits for them, and re-layouts: 382 us -> 469 us
    ppermute x0 -> x30, waiting for transfers between devices: none -> 267 us  [kron_apply(): lax.ppermute(ring[-1], 'pts', [(dev, (dev + 1) % 16) for dev in range(16)])]
    all_gather x2 -> x0, waiting for transfers between devices: 71.9 us -> none  [kron_apply(): gathered = lax.all_gather(partial_value, 'pts', axis=1, tiled=True)]
    unnamed x22 -> x138, local copies, waits for them, and re-layouts: 6.09 us -> 69.7 us
    dynamic_slice x0 -> x2, local copies, waits for them, and re-layouts: none -> 23.3 us  [kron_apply(): jnp.roll(jnp.concatenate(ring[::-1], axis=1), (lax.axis_index('pts') + 1)...]
  transfers between devices with their start and end apart: 3 -> 31, of which waited for: 3 -> 30; matrix products, arithmetic and copies ran while one was open for 2% -> 2% of each run, Pallas kernels for 0% -> 0%
where the time goes in v1:
time: 1280 us; the launch traced here: 1270 us
  local copies, waits for them, and re-layouts  469 us (37%)
  waiting for transfers between devices  368 us (29%)
  other arithmetic  343 us (27%)
  matrix products  39 us (3%)
  blocking collectives  34 us (3%)
  between operations  16.2 us (1%)
    gather x2, local copies, waits for them, and re-layouts, pick_cells(): taken = jnp.take(grid_rows, row_ids, axis=1)  330 us
    ppermute x30, waiting for transfers between devices, kron_apply(): lax.ppermute(ring[-1], 'pts', [(dev, (dev + 1) % 16) for dev in range(16)])  267 us
    scatter-add x1, other arithmetic, slab_add(): jnp.zeros((row_count * size_y, size_z), jnp.float32).at[target_row]  199 us
    reduce_sum x2, other arithmetic, pick_cells(): return jnp.sum(kept.astype(jnp.float32), axis=-1).astype(jnp.bfloat16)  114 us
    reduce_scatter x1, waiting for transfers between devices, body(): lax.psum_scatter(slab_add(flat_rows, flat_depths, flat_terms, slab_rows *...  101 us
    unnamed x138, local copies, waits for them, and re-layouts  69.7 us
    psum x1, blocking collectives, body(): loglik, descent = lax.psum((loglik_local, descent_local), 'pts')  34 us
  transfers between devices with their start and end apart: 31, of which 30 were waited for; matrix products, arithmetic and copies ran while one was open for 2% of the time, Pallas kernels for 0%

profile of v1, /device:TPU:0, one launch (start us, length us, event | category | flops | bytes accessed | tf_op | source)
XLA Modules:
  0.0 1270.3 jit_solution(9295334030271554988)
XLA Ops:
  7.2 2.3 fusion.16
  11.9 11.8 collective-permute-done
  23.8 11.3 collective-permute-done.1
  35.1 11.3 collective-permute-done.2
  46.4 11.3 collective-permute-done.3
  57.7 11.3 collective-permute-done.4
  69.0 11.3 collective-permute-done.5
  81.1 11.3 collective-permute-done.6
  93.2 11.3 collective-permute-done.7
  105.3 11.3 collective-permute-done.8
  117.5 11.3 collective-permute-done.9
  131.7 9.2 collective-permute-done.10
  143.5 9.5 collective-permute-done.11
  153.1 6.5 iota_compare_fusion.1
  159.5 5.2 collective-permute-done.12
  168.4 7.9 collective-permute-done.13
  177.2 10.6 collective-permute-done.14
  188.7 2.0 constant_dynamic-update-slice_fusion.30
  190.7 1.9 constant_dynamic-update-slice_fusion.29
  192.6 1.9 constant_dynamic-update-slice_fusion.28
  194.6 2.0 constant_dynamic-update-slice_fusion.27
  196.6 2.0 constant_dynamic-update-slice_fusion.26
  198.6 2.0 constant_dynamic-update-slice_fusion.25
  200.7 2.0 constant_dynamic-update-slice_fusion.24
  210.7 1.9 constant_dynamic-update-slice_fusion.14
  212.6 1.9 constant_dynamic-update-slice_fusion.13
  214.6 2.0 constant_dynamic-update-slice_fusion.12
  227.2 10.4 constant_dynamic-slice_fusion
  237.6 12.9 %copy.45 = bf16[2,128,128,128]{3,1,2,0:T(8,128)(2,1)} copy(bf16[2,128,128,128]{2,3,1,0:T(8,128)(2,1)} %constant_dynamic-slice_fusion) | data formatting | bytes 16777216 | tf_op jit(solution)/shard_map/jit(_roll_dynamic)/dynamic_slice | solution.py:61
  250.5 9.7 fusion.37
  260.2 5.7 copy-done.1
  266.0 4.1 convert_bitcast_fusion
  270.1 12.1 copy.46
  282.2 16.4 %copy.47 = bf16[2,16384,128]{2,0,1:T(2,128)(2,1)} copy(bf16[2,16384,128]{2,1,0:T(8,128)(2,1)} %bitcast.119) | data formatting | bytes 16777216 | tf_op jit(solution)/shard_map/reshape | solution.py:97
  298.6 216.7 %gather_fusion = bf16[32768,2,128]{2,1,0:T(2,128)(2,1)} fusion(bf16[2,16384,128]{2,0,1:T(2,128)(2,1)} %copy.47, s32[32768]{0:T(1024)S(1)} %broadcast_clamp_fusion), kind=kCustom, calls=%fused_computation | custom fusion | bytes 33685504 | tf_op jit(solution)/shard_map/jit(_take)/gather | solution.py:37
  515.3 97.9 %fusion.2 = bf16[128,256,2]{2,1,0:T(8,128)(2,1)} fusion(bf16[128,256,2,128]{3,2,1,0:T(2,128)(2,1)} %bitcast.116, pred[128,256]{1,0:T(8,128)(4,1)S(1)} %get-tuple-element.15, pred[128,256,128]{2,1,0:T(8,128)(4,1)} %iota_compare_fusion.1), kind=kLoop, calls=%fused_computation.10 | loop fusion | flops 25100288 | bytes 21135360 | tf_op jit(solution)/shard_map/reduce_sum | solution.py:41
  613.2 8.1 fusion.13
  622.8 4.6 fusion.45
  627.5 198.8 %scatter_custom_fusion = f32[16384,128]{1,0:T(8,128)} fusion(s32[32768]{0:T(1024)} %bitcast.136, f32[]{:T(128)} %constant.118.clone.1, f32[32768]{0:T(1024)S(1)} %bitcast.131, s32[32768]{0:T(1024)S(1)} %bitcast.130), kind=kCustom, calls=%fused_computation.6 | custom fusion | flops 12582912 | bytes 8651776 | tf_op jit(solution)/shard_map/scatter-add | solution.py:50
  826.4 101.3 %reduce-scatter.2.cloned.1.call-done = f32[8,128,128]{2,1,0:T(8,128)} async-done(((f32[128,128,128]{2,1,0:T(8,128)}), f32[8,128,128]{2,1,0:T(8,128)}) %reduce-scatter.2.cloned.1.call-update) | async-done | bytes 524304 | tf_op jit(solution)/shard_map/reduce_scatter | solution.py:123
  927.6 2.6 fusion.50
  931.5 8.5 collective-permute-done.15
  940.0 8.5 collective-permute-done.16
  948.5 8.5 collective-permute-done.17
  957.0 8.5 collective-permute-done.18
  965.5 8.5 collective-permute-done.19
  973.9 8.5 collective-permute-done.20
  983.4 8.5 collective-permute-done.21
  992.6 8.5 collective-permute-done.22
  1001.8 8.5 collective-permute-done.23
  1011.0 8.5 collective-permute-done.24
  1020.2 8.6 collective-permute-done.25
  1030.3 7.3 collective-permute-done.26
  1041.3 5.1 collective-permute-done.27
  1049.6 34.0 %all-reduce = (f32[5]{0:T(128)S(1)}, f32[3]{0:T(128)S(1)}, f32[5]{0:T(128)S(1)}) all-reduce(f32[5]{0:T(128)} %neg.22, f32[3]{0:T(128)S(1)} %pad_maximum_fusion, f32[5]{0:T(128)} %get-tuple-element.8), channel_id=1, replica_groups=mesh['parts'=2,'pts'=16] {'pts'}, use_global_device_ids=true, to_apply=%region_6.7 | all-reduce | flops 13 | bytes 104 | tf_op jit(solution)/shard_map/psum | solution.py:108
  1084.8 2.3 subtract_multiply_fusion.1
  1087.1 5.3 collective-permute-done.29
  1108.0 2.3 dynamic-slice_bitcast_fusion
  1110.3 6.7 copy.52
  1117.0 5.6 convert_bitcast_fusion.1
  1122.6 4.7 copy.53
  1127.4 113.0 %gather_fusion.1 = bf16[32768,128]{1,0:T(8,128)(2,1)} fusion(bf16[16384,128]{1,0:T(8,128)(2,1)} %bitcast.115, s32[32768]{0:T(1024)S(1)} %broadcast_clamp_fusion), kind=kCustom, calls=%fused_computation.1 | custom fusion | bytes 16908288 | tf_op jit(solution)/shard_map/jit(_take)/gather | solution.py:37
  1240.3 15.8 %fusion.4 = bf16[128,256]{1,0:T(8,128)(2,1)S(1)} fusion(bf16[1,128,256,128]{3,2,1,0:T(8,128)(2,1)} %bitcast.117, s32[128,256]{1,0:T(8,128)S(1)} %fusion.30, pred[128,256]{1,0:T(8,128)(4,1)S(1)} %copy-done.31), kind=kLoop, calls=%fused_computation.12 | loop fusion | flops 16744448 | bytes 8617984 | tf_op jit(solution)/shard_map/reduce_sum | solution.py:41
  1256.1 5.6 fusion.31
  (184 shorter events, 67.1 us)
Async XLA Ops:
  7.2 243.3 %copy-start = (f32[128,128]{1,0:T(8,128)S(1)}, f32[128,128]{1,0:T(8,128)}, u32[]{:S(2)}) copy-start(f32[128,128]{1,0:T(8,128)} %param.13) | copy-start | bytes 196612
  7.2 159.8 %copy-start.17 = (s32[128,256]{1,0:T(8,128)S(1)}, s32[128,256]{1,0:T(8,128)}, u32[]{:S(2)}) copy-start(s32[128,256]{1,0:T(8,128)} %param.18) | copy-start | bytes 393220
  7.2 160.6 %copy-start.35 = (f32[5]{0:T(128)S(1)}, f32[5]{0:T(128)}, u32[]{:S(2)}) copy-start(f32[5]{0:T(128)} %param.20) | copy-start | bytes 64
  7.2 920.4 %reduce-scatter.2.cloned.1.call-start = ((), (), s32[]{:S(2)}) async-start(), calls=%async_computation.1 | async-start | bytes 8912896 | tf_op jit(solution)/shard_map/reduce_scatter | solution.py:123
  11.4 12.4 collective-permute-start
  23.8 11.3 collective-permute-start.1
  35.1 11.3 collective-permute-start.2
  46.4 11.3 collective-permute-start.3
  57.7 11.3 collective-permute-start.4
  69.0 11.3 collective-permute-start.5
  80.3 0.8 copy-start.4
  81.1 11.3 collective-permute-start.6
  92.4 0.8 copy-start.6
  93.2 11.3 collective-permute-start.7
  104.5 0.8 copy-start.8
  105.3 11.3 collective-permute-start.8
  116.6 0.8 copy-start.10
  117.5 11.3 collective-permute-start.9
  128.8 0.8 copy-start.12
  129.6 11.3 collective-permute-start.10
  131.5 21.6 %copy-start.18 = (s32[128,256]{1,0:T(8,128)}, s32[128,256]{1,0:T(8,128)S(1)}, u32[]{:S(2)}) copy-start(s32[128,256]{1,0:T(8,128)S(1)} %get-tuple-element.16) | copy-start | bytes 393220
  131.5 383.8 %copy-start.30 = (pred[128,256]{1,0:T(8,128)(4,1)}, pred[128,256]{1,0:T(8,128)(4,1)S(1)}, u32[]{:S(2)}) copy-start(pred[128,256]{1,0:T(8,128)(4,1)S(1)} %get-tuple-element.15) | copy-start | bytes 98308
  140.9 0.8 copy-start.14
  141.7 11.4 collective-permute-start.11
  153.1 11.6 collective-permute-start.12
  164.7 11.6 collective-permute-start.13
  167.8 34.9 %copy-start.7 = (bf16[2,8,128,128]{2,3,1,0:T(8,128)(2,1)S(1)}, bf16[2,8,128,128]{2,3,1,0:T(8,128)(2,1)}, u32[]{:S(2)}) copy-start(bf16[2,8,128,128]{2,3,1,0:T(8,128)(2,1)} %copy-done.6) | copy-start | bytes 1572868
  167.8 35.8 %copy-start.5 = (bf16[2,8,128,128]{2,3,1,0:T(8,128)(2,1)S(1)}, bf16[2,8,128,128]{2,3,1,0:T(8,128)(2,1)}, u32[]{:S(2)}) copy-start(bf16[2,8,128,128]{2,3,1,0:T(8,128)(2,1)} %copy-done.4) | copy-start | bytes 1572868
  176.3 11.5 collective-permute-start.14
  194.6 22.0 %copy-start.15 = (bf16[2,8,128,128]{2,3,1,0:T(8,128)(2,1)S(1)}, bf16[2,8,128,128]{2,3,1,0:T(8,128)(2,1)}, u32[]{:S(2)}) copy-start(bf16[2,8,128,128]{2,3,1,0:T(8,128)(2,1)} %copy-done.14) | copy-start | bytes 1572868
  196.6 20.8 %copy-start.13 = (bf16[2,8,128,128]{2,3,1,0:T(8,128)(2,1)S(1)}, bf16[2,8,128,128]{2,3,1,0:T(8,128)(2,1)}, u32[]{:S(2)}) copy-start(bf16[2,8,128,128]{2,3,1,0:T(8,128)(2,1)} %copy-done.12) | copy-start | bytes 1572868
  198.6 19.7 %copy-start.11 = (bf16[2,8,128,128]{2,3,1,0:T(8,128)(2,1)S(1)}, bf16[2,8,128,128]{2,3,1,0:T(8,128)(2,1)}, u32[]{:S(2)}) copy-start(bf16[2,8,128,128]{2,3,1,0:T(8,128)(2,1)} %copy-done.10) | copy-start | bytes 1572868
  200.7 18.6 %copy-start.9 = (bf16[2,8,128,128]{2,3,1,0:T(8,128)(2,1)S(1)}, bf16[2,8,128,128]{2,3,1,0:T(8,128)(2,1)}, u32[]{:S(2)}) copy-start(bf16[2,8,128,128]{2,3,1,0:T(8,128)(2,1)} %copy-done.8) | copy-start | bytes 1572868
  260.2 5.8 copy-start.1
  613.2 8.2 copy-start.33
  621.4 1.3 copy-start.27
  622.8 4.7 copy-start.29
  627.5 300.1 %copy-start.2 = (f32[8,128,128]{2,1,0:T(8,128)S(1)}, f32[8,128,128]{2,1,0:T(8,128)}, u32[]{:S(2)}) copy-start(f32[8,128,128]{2,1,0:T(8,128)} %param.12) | copy-start | bytes 1572868
  627.5 300.1 %copy-start.3 = (f32[8,128,128]{2,1,0:T(8,128)S(1)}, f32[8,128,128]{2,1,0:T(8,128)}, u32[]{:S(2)}) copy-start(f32[8,128,128]{2,1,0:T(8,128)} %param.11) | copy-start | bytes 1572868
  627.5 302.7 %copy-start.32 = (f32[128,128]{1,0:T(8,128)S(1)}, f32[128,128]{1,0:T(8,128)}, u32[]{:S(2)}) copy-start(f32[128,128]{1,0:T(8,128)} %param.15) | copy-start | bytes 196612
  627.5 303.3 %copy-start.34 = (f32[128,128]{1,0:T(8,128)S(1)}, f32[128,128]{1,0:T(8,128)}, u32[]{:S(2)}) copy-start(f32[128,128]{1,0:T(8,128)} %param.14) | copy-start | bytes 196612
  930.2 173.4 %copy-start.16 = (f32[8,128,128]{2,1,0:T(8,128)}, f32[8,128,128]{2,1,0:T(8,128)S(1)}, u32[]{:S(2)}) copy-start(f32[8,128,128]{2,1,0:T(8,128)S(1)} %get-tuple-element.13) | copy-start | bytes 1572868
  931.4 8.5 collective-permute-start.15
  940.0 8.5 collective-permute-start.16
  948.5 8.5 collective-permute-start.17
  957.0 8.5 collective-permute-start.18
  965.4 8.5 collective-permute-start.19
  973.9 8.5 collective-permute-start.20
  982.4 0.7 copy-start.19
  983.2 8.7 collective-permute-start.21
  991.8 0.7 copy-start.20
  992.6 8.5 collective-permute-start.22
  1001.8 8.5 collective-permute-start.23
  1011.0 8.5 collective-permute-start.24
  1020.2 8.6 collective-permute-start.25
  1028.8 8.8 collective-permute-start.26
  1037.6 8.8 collective-permute-start.27
  1046.4 37.2 %collective-permute-start.28 = (bf16[1,8,128,128]{2,3,1,0:T(8,128)(2,1)}, bf16[1,8,128,128]{2,3,1,0:T(8,128)(2,1)}, u32[]{:S(2)}, u32[]{:S(2)}) collective-permute-start(bf16[1,8,128,128]{2,3,1,0:T(8,128)(2,1)} %collective-permute-done.27), channel_id=1, source_target_pairs={{0,1},{1,2},{2,3},{3,4},{4,5},{5,6},{6,7},{7,8},{8,9},{9,10},{10,1... | collective-permute-start | bytes 786440 | tf_op jit(solution)/shard_map/ppermute | solution.py:60
  1047.7 57.9 %copy-start.26 = (bf16[1,8,128,128]{2,3,1,0:T(8,128)(2,1)S(1)}, bf16[1,8,128,128]{2,3,1,0:T(8,128)(2,1)}, u32[]{:S(2)}) copy-start(bf16[1,8,128,128]{2,3,1,0:T(8,128)(2,1)} %copy-done.25) | copy-start | bytes 786436
  1047.7 58.0 %copy-start.24 = (bf16[1,8,128,128]{2,3,1,0:T(8,128)(2,1)S(1)}, bf16[1,8,128,128]{2,3,1,0:T(8,128)(2,1)}, u32[]{:S(2)}) copy-start(bf16[1,8,128,128]{2,3,1,0:T(8,128)(2,1)} %copy-done.23) | copy-start | bytes 786436
  1047.7 58.0 %copy-start.22 = (bf16[1,8,128,128]{2,3,1,0:T(8,128)(2,1)S(1)}, bf16[1,8,128,128]{2,3,1,0:T(8,128)(2,1)}, u32[]{:S(2)}) copy-start(bf16[1,8,128,128]{2,3,1,0:T(8,128)(2,1)} %copy-done.21) | copy-start | bytes 786436
  1083.6 8.7 collective-permute-start.29
  1127.4 113.0 %copy-start.31 = (pred[128,256]{1,0:T(8,128)(4,1)S(1)}, pred[128,256]{1,0:T(8,128)(4,1)}, u32[]{:S(2)}) copy-start(pred[128,256]{1,0:T(8,128)(4,1)} %copy-done.30) | copy-start | bytes 98308
  1240.3 21.4 %copy-start.28 = (f32[1,128,128]{2,0,1:T(1,128)S(1)}, f32[1,128,128]{2,0,1:T(1,128)}, u32[]{:S(2)}) copy-start(f32[1,128,128]{2,0,1:T(1,128)} %copy-done.27) | copy-start | bytes 196612
  (3 other events, 2.2 us)
Sparse Core Ops, SparseCore 0:
  826.5 101.1 reduce-scatter.1
